TPU v7x, 32 devices: a whole 2x2x4 slice. The times are simulated.
32 devices in a mesh: sub: 8 (over y, x, core), col: 4 (over z).
Axes of the slice: x: 2, y: 2, z: 4, core: 2. Of those that a mesh axis runs over, the one named last changes fastest.
Arguments:
- state_init: float32 [128, 8192], P('col', 'sub'), may hold values from -3 to 3
- load_cols: float32 [128, 8192], P('col', 'sub'), may hold values from -6 to 6
- stiff_diag: bfloat16 [1024, 8192], P(None, 'sub'), may hold values from -0.1875 to 0.1875
- stiff_rim: bfloat16 [1024, 8192], P(None, 'sub'), may hold values from -0.1875 to 0.1875
- inverse: bfloat16 [2048, 8192], P(None, 'sub'), may hold values from -0.125 to 0.125
- ov_rows: int32 [8, 1024], P('sub'), may hold values from 0 to 1023, as said below
- ov_count: int32 [8], P('sub'), may hold values from 512 to 1024, as said below
- coarse_basis: bfloat16 [8192, 192], P('sub'), may hold values from -0.1875 to 0.1875
- coarse_map: bfloat16 [1536, 1536], P('sub', 'col'), may hold values from -0.21875 to 0.21875
Outputs:
- solution: float32 [128, 8192], P('col', 'sub')
- residual: float32 [128, 8192], P('col', 'sub')
Inputs may be any that keep to these rules, and one draw needn't show every extreme that they name: `ov_rows`: each row holds 1024 different rim positions. `ov_count`: some subdomain uses all 1024 margin slots in every draw.
All inputs are finite; a program needn't handle non-finite values.
Results may differ from a plain program's by a relative error of at most 0.0075.
Values may be sent and summed in bfloat16 or wider, within the bound.
A program may use at most 64 MiB of HBM per device.

v0:
```python
import jax
import jax.numpy as jnp
from jax import lax
from jax.sharding import PartitionSpec as P

H = 512
ITERS = 2


cubic_coef = 0.1


def with_halo(cells, sides, width):
    for axis, dim in sides:
        count = lax.axis_size(axis)
        ends = count - 1
        head = lax.slice_in_dim(cells, 0, width, axis=dim)
        tail = lax.slice_in_dim(cells, cells.shape[dim] - width, cells.shape[dim], axis=dim)
        cells = jnp.concatenate(
            [
                lax.ppermute(tail, axis, [(i, (i + 1) % count) for i in range(ends)]),
                cells,
                lax.ppermute(head, axis, [((i + 1) % count, i) for i in range(ends)]),
            ],
            axis=dim,
        )
    return cells


def residual_of(current, load_cols, stiff_diag, stiff_rim):
    rounded = current.astype(jnp.bfloat16)
    padded = with_halo(rounded, (("sub", 1),), H)
    border = jnp.concatenate([padded[:, :H], padded[:, padded.shape[1] - H :]], axis=1)
    applied = jnp.dot(rounded, stiff_diag, preferred_element_type=jnp.float32)
    applied = applied + jnp.dot(border, stiff_rim, preferred_element_type=jnp.float32)
    return load_cols - applied - cubic_coef * current * current * current


def body(
    state_init,
    load_cols,
    stiff_diag,
    stiff_rim,
    inverse,
    ov_rows,
    ov_count,
    coarse_basis,
    coarse_map,
):
    current = state_init
    width_coarse = coarse_basis.shape[1]
    slots = ov_rows.shape[1]
    col_count = lax.axis_size("col")
    sub_count = lax.axis_size("sub")
    per_block = width_coarse // col_count
    load_rows = current.shape[0]
    live = lax.broadcasted_iota(jnp.int32, (1, slots), 1) < ov_count[0]
    for iteration in range(ITERS):
        residual_now = residual_of(current, load_cols, stiff_diag, stiff_rim)
        rounded = residual_now.astype(jnp.bfloat16)
        padded = with_halo(rounded, (("sub", 1),), H)
        border = jnp.concatenate([padded[:, :H], padded[:, padded.shape[1] - H :]], axis=1)
        picked = jnp.take(border, ov_rows[0], axis=1)
        picked = jnp.where(live, picked, jnp.zeros_like(picked))
        local_rhs = jnp.concatenate([rounded, picked], axis=1)
        fine_part = jnp.dot(local_rhs, inverse, preferred_element_type=jnp.float32)
        coefficients = jnp.dot(rounded, coarse_basis, preferred_element_type=jnp.float32).astype(
            jnp.bfloat16
        )
        partial_sums = jnp.dot(
            lax.all_gather(coefficients, "col", axis=0, tiled=True),
            coarse_map,
            preferred_element_type=jnp.float32,
        )
        totals = lax.psum(partial_sums, "sub")
        own_total = lax.all_to_all(
            totals.astype(jnp.bfloat16), "col", split_axis=0, concat_axis=1, tiled=True
        ).astype(totals.dtype)
        arranged = own_total.reshape(load_rows, col_count, sub_count, per_block)
        coarse = lax.dynamic_index_in_dim(arranged, lax.axis_index("sub"), 2, keepdims=False)
        coarse = coarse.reshape(load_rows, width_coarse)
        coarse = coarse.astype(jnp.bfloat16)
        coarse_lift = lax.dot_general(
            coarse, coarse_basis, (((1,), (1,)), ((), ())), preferred_element_type=jnp.float32
        )
        current = current + (fine_part + coarse_lift)
    final_residual = residual_of(current, load_cols, stiff_diag, stiff_rim)
    return (current, final_residual)


def solution(mesh):
    in_specs = (
        P("col", "sub"),
        P("col", "sub"),
        P(None, "sub"),
        P(None, "sub"),
        P(None, "sub"),
        P("sub", None),
        P("sub"),
        P("sub", None),
        P("sub", "col"),
    )
    out_specs = (P("col", "sub"), P("col", "sub"))
    return jax.shard_map(body, mesh=mesh, in_specs=in_specs, out_specs=out_specs, check_vma=False)
```

profile of v0, /device:TPU:11, one launch (start us, length us, event | category | flops | bytes accessed | tf_op | source)
XLA Modules:
  0.0 148.7 jit_solution(11905040138602207513)
XLA Ops:
  0.6 0.0 copy-start
  0.7 1.1 convert_element_type.59
  1.7 3.7 %collective-permute-start = (bf16[32,512]{1,0:T(8,128)(2,1)S(1)}, bf16[32,512]{1,0:T(8,128)(2,1)S(1)}, u32[]{:S(2)}, u32[]{:S(2)}) collective-permute-start(bf16[32,512]{1,0:T(8,128)(2,1)S(1)} %get-tuple-element.11), channel_id=1, source_target_pairs={{0,4},{4,8},{8,12},{12,16},{16,20},{20,24},{24,28},{1,5},{5,9},{9,... | collective-permute-start | bytes 98312 | tf_op jit(solution)/shard_map/ppermute | solution.py:21
  5.4 0.0 copy-start.3
  5.4 2.1 %collective-permute-start.1 = (bf16[32,512]{1,0:T(8,128)(2,1)S(1)}, bf16[32,512]{1,0:T(8,128)(2,1)S(1)}, u32[]{:S(2)}, u32[]{:S(2)}) collective-permute-start(bf16[32,512]{1,0:T(8,128)(2,1)S(1)} %get-tuple-element.12), channel_id=1, source_target_pairs={{4,0},{8,4},{12,8},{16,12},{20,16},{24,20},{28,24},{5,1},{9,5},{13... | collective-permute-start | bytes 98312 | tf_op jit(solution)/shard_map/ppermute | solution.py:23
  7.5 0.5 fusion.40
  8.0 0.0 copy-done.9
  8.0 0.0 copy-start.8
  8.7 0.0 copy-start.10
  8.8 0.0 collective-permute-done
  8.8 3.0 %collective-permute-done.1 = bf16[32,512]{1,0:T(8,128)(2,1)S(1)} collective-permute-done((bf16[32,512]{1,0:T(8,128)(2,1)S(1)}, bf16[32,512]{1,0:T(8,128)(2,1)S(1)}, u32[]{:S(2)}, u32[]{:S(2)}) %collective-permute-start.1) | collective-permute-done | bytes 32800 | tf_op jit(solution)/shard_map/ppermute | solution.py:23
  11.7 2.1 %fusion.8 = bf16[32,1024]{1,0:T(8,128)(2,1)S(1)} fusion(f32[32,1024]{1,0:T(8,128)S(1)} %copy-done.5, f32[32,1024]{1,0:T(8,128)S(1)} %fusion.40, bf16[1024,1024]{1,0:T(8,128)(2,1)} %param.14, f32[32,1024]{1,0:T(8,128)S(1)} %copy-done.4, bf16[32,512]{1,0:T(8,128)(2,1)S(1)} %collective-permute-done.1, bf16[32,512]{1,0:T(8,128)(2,1)S(1)} %collective-permute-done), kind=kOutput, calls=%fused_computation.15 | convolution fusion | flops 67469312 | bytes 2621440 | tf_op jit(solution)/shard_map/dot_general | solution.py:35
  13.8 1.9 %collective-permute-start.2 = (bf16[32,512]{1,0:T(8,128)(2,1)S(1)}, bf16[32,512]{1,0:T(8,128)(2,1)S(1)}, u32[]{:S(2)}, u32[]{:S(2)}) collective-permute-start(bf16[32,512]{1,0:T(8,128)(2,1)S(1)} %get-tuple-element.9), channel_id=1, source_target_pairs={{0,4},{4,8},{8,12},{12,16},{16,20},{20,24},{24,28},{1,5},{5,9},{9,... | collective-permute-start | bytes 98312 | tf_op jit(solution)/shard_map/ppermute | solution.py:21
  15.8 2.4 %collective-permute-start.3 = (bf16[32,512]{1,0:T(8,128)(2,1)S(1)}, bf16[32,512]{1,0:T(8,128)(2,1)S(1)}, u32[]{:S(2)}, u32[]{:S(2)}) collective-permute-start(bf16[32,512]{1,0:T(8,128)(2,1)S(1)} %get-tuple-element.10), channel_id=1, source_target_pairs={{4,0},{8,4},{12,8},{16,12},{20,16},{24,20},{28,24},{5,1},{9,5},{13... | collective-permute-start | bytes 98312 | tf_op jit(solution)/shard_map/ppermute | solution.py:23
  18.2 0.2 convolution_convert_fusion.1
  18.4 10.5 %all_gather.6 = bf16[128,192]{1,0:T(8,128)(2,1)S(1)} all-gather(bf16[32,192]{1,0:T(8,128)(2,1)S(1)} %convolution_convert_fusion.1), channel_id=1, replica_groups=mesh['sub'=8,'col'=4] {'col'}, dimensions={0}, use_global_device_ids=true | all-gather | bytes 61440 | tf_op jit(solution)/shard_map/all_gather | solution.py:71
  28.9 0.2 fusion.41
  29.1 27.4 %all-reduce.2 = bf16[128,384]{1,0:T(8,128)(2,1)} all-reduce(f32[128,384]{1,0:T(8,128)S(1)} %fusion.41), channel_id=1, replica_groups=mesh['sub'=8,'col'=4] {'sub'}, use_global_device_ids=true, to_apply=%region_0.0 | all-reduce | flops 49152 | bytes 294912 | tf_op jit(solution)/shard_map/psum | solution.py:75
  56.4 4.5 %all-to-all-start = ((bf16[4,32,384]{2,1,0:T(8,128)(2,1)}), bf16[4,32,384]{2,1,0:T(8,128)(2,1)}, u32[]{:S(2)}, u32[]{:S(2)}) async-start(bf16[4,32,384]{2,1,0:T(8,128)(2,1)} %bitcast.3), calls=%async_computation | async-start | bytes 196608 | tf_op jit(solution)/shard_map/all_to_all | solution.py:76
  61.0 0.0 collective-permute-done.2
  61.0 0.0 collective-permute-done.3
  61.0 0.2 copy.19
  61.2 3.2 %gather_fusion = bf16[1024,32]{1,0:T(8,128)(2,1)S(1)} fusion(bf16[32,1024]{0,1:T(8,128)(2,1)S(1)} %copy.19, s32[1024]{0:T(1024)S(1)} %fusion.27), kind=kCustom, calls=%fused_computation.clone | custom fusion | bytes 135168 | tf_op jit(solution)/shard_map/jit(_take)/gather | solution.py:63
  64.4 0.1 copy.20
  64.6 3.0 %fusion.10 = f32[32,1024]{1,0:T(8,128)S(1)} fusion(bf16[2048,1024]{1,0:T(8,128)(2,1)} %param.15, bf16[32,1024]{1,0:T(8,128)(2,1)S(1)} %bitcast_select_fusion.1, bf16[32,1024]{1,0:T(8,128)(2,1)S(1)} %fusion.8), kind=kOutput, calls=%fused_computation.24 | convolution fusion | flops 134479872 | bytes 4456448 | tf_op jit(solution)/shard_map/dot_general | solution.py:66
  67.6 0.0 all-to-all-done
  67.6 1.1 reshape.34
  68.7 0.1 dynamic-slice_convert_fusion.1
  68.9 0.1 convert_element_type.67
  69.0 0.0 copy-start.1
  69.0 0.2 fusion.38
  69.2 5.1 %collective-permute-start.4 = (bf16[32,512]{1,0:T(8,128)(2,1)S(1)}, bf16[32,512]{1,0:T(8,128)(2,1)S(1)}, u32[]{:S(2)}, u32[]{:S(2)}) collective-permute-start(bf16[32,512]{1,0:T(8,128)(2,1)S(1)} %get-tuple-element.7), channel_id=1, source_target_pairs={{0,4},{4,8},{8,12},{12,16},{16,20},{20,24},{24,28},{1,5},{5,9},{9,... | collective-permute-start | bytes 98312 | tf_op jit(solution)/shard_map/ppermute | solution.py:21
  74.3 1.9 %collective-permute-start.5 = (bf16[32,512]{1,0:T(8,128)(2,1)S(1)}, bf16[32,512]{1,0:T(8,128)(2,1)S(1)}, u32[]{:S(2)}, u32[]{:S(2)}) collective-permute-start(bf16[32,512]{1,0:T(8,128)(2,1)S(1)} %get-tuple-element.8), channel_id=1, source_target_pairs={{4,0},{8,4},{12,8},{16,12},{20,16},{24,20},{28,24},{5,1},{9,5},{13... | collective-permute-start | bytes 98312 | tf_op jit(solution)/shard_map/ppermute | solution.py:23
  76.2 0.5 fusion.42
  76.7 0.0 collective-permute-done.4
  76.7 3.7 %collective-permute-done.5 = bf16[32,512]{1,0:T(8,128)(2,1)S(1)} collective-permute-done((bf16[32,512]{1,0:T(8,128)(2,1)S(1)}, bf16[32,512]{1,0:T(8,128)(2,1)S(1)}, u32[]{:S(2)}, u32[]{:S(2)}) %collective-permute-start.5) | collective-permute-done | bytes 32800 | tf_op jit(solution)/shard_map/ppermute | solution.py:23
  80.4 0.5 fusion.9
  80.9 0.2 convolution_convert_fusion
  81.1 1.9 %collective-permute-start.6 = (bf16[32,512]{1,0:T(8,128)(2,1)S(1)}, bf16[32,512]{1,0:T(8,128)(2,1)S(1)}, u32[]{:S(2)}, u32[]{:S(2)}) collective-permute-start(bf16[32,512]{1,0:T(8,128)(2,1)S(1)} %get-tuple-element.5), channel_id=1, source_target_pairs={{0,4},{4,8},{8,12},{12,16},{16,20},{20,24},{24,28},{1,5},{5,9},{9,... | collective-permute-start | bytes 98312 | tf_op jit(solution)/shard_map/ppermute | solution.py:21
  83.1 2.4 %collective-permute-start.7 = (bf16[32,512]{1,0:T(8,128)(2,1)S(1)}, bf16[32,512]{1,0:T(8,128)(2,1)S(1)}, u32[]{:S(2)}, u32[]{:S(2)}) collective-permute-start(bf16[32,512]{1,0:T(8,128)(2,1)S(1)} %get-tuple-element.6), channel_id=1, source_target_pairs={{4,0},{8,4},{12,8},{16,12},{20,16},{24,20},{28,24},{5,1},{9,5},{13... | collective-permute-start | bytes 98312 | tf_op jit(solution)/shard_map/ppermute | solution.py:23
  85.5 10.2 %all_gather.7 = bf16[128,192]{1,0:T(8,128)(2,1)S(1)} all-gather(bf16[32,192]{1,0:T(8,128)(2,1)S(1)} %convolution_convert_fusion), channel_id=1, replica_groups=mesh['sub'=8,'col'=4] {'col'}, dimensions={0}, use_global_device_ids=true | all-gather | bytes 61440 | tf_op jit(solution)/shard_map/all_gather | solution.py:71
  95.7 0.2 fusion.43
  95.9 27.4 %all-reduce.3 = bf16[128,384]{1,0:T(8,128)(2,1)} all-reduce(f32[128,384]{1,0:T(8,128)S(1)} %fusion.43), channel_id=1, replica_groups=mesh['sub'=8,'col'=4] {'sub'}, use_global_device_ids=true, to_apply=%region_1.3 | all-reduce | flops 49152 | bytes 294912 | tf_op jit(solution)/shard_map/psum | solution.py:75
  123.4 4.6 %all-to-all-start.1 = ((bf16[4,32,384]{2,1,0:T(8,128)(2,1)}), bf16[4,32,384]{2,1,0:T(8,128)(2,1)S(1)}, u32[]{:S(2)}, u32[]{:S(2)}) async-start(bf16[4,32,384]{2,1,0:T(8,128)(2,1)} %bitcast.6), calls=%async_computation.1 | async-start | bytes 196608 | tf_op jit(solution)/shard_map/all_to_all | solution.py:76
  127.9 0.0 collective-permute-done.6
  127.9 0.0 collective-permute-done.7
  127.9 0.2 copy.22
  128.1 3.7 %gather_fusion.1 = bf16[1024,32]{1,0:T(8,128)(2,1)S(1)} fusion(bf16[32,1024]{0,1:T(8,128)(2,1)S(1)} %copy.22, s32[1024]{0:T(1024)} %copy-done.8), kind=kCustom, calls=%fused_computation.1.clone | custom fusion | bytes 135168 | tf_op jit(solution)/shard_map/jit(_take)/gather | solution.py:63
  131.8 0.1 copy.23
  131.9 0.7 bitcast_select_fusion
  132.6 3.0 %fusion.14 = f32[32,1024]{1,0:T(8,128)S(1)} fusion(bf16[2048,1024]{1,0:T(8,128)(2,1)} %param.15, bf16[32,1024]{1,0:T(8,128)(2,1)S(1)} %bitcast_select_fusion, bf16[32,1024]{1,0:T(8,128)(2,1)S(1)} %fusion.9), kind=kOutput, calls=%fused_computation.28 | convolution fusion | flops 134479872 | bytes 4456448 | tf_op jit(solution)/shard_map/dot_general | solution.py:66
  135.6 0.0 all-to-all-done.1
  135.6 0.2 reshape.35
  135.9 0.1 dynamic-slice_convert_fusion
  136.0 0.1 convert_element_type.76
  136.1 0.0 copy-start.2
  136.1 0.2 fusion.39
  136.3 0.0 copy-start.7
  136.3 5.1 %collective-permute-start.8 = (bf16[32,512]{1,0:T(8,128)(2,1)S(1)}, bf16[32,512]{1,0:T(8,128)(2,1)S(1)}, u32[]{:S(2)}, u32[]{:S(2)}) collective-permute-start(bf16[32,512]{1,0:T(8,128)(2,1)S(1)} %get-tuple-element.3), channel_id=1, source_target_pairs={{0,4},{4,8},{8,12},{12,16},{16,20},{20,24},{24,28},{1,5},{5,9},{9,... | collective-permute-start | bytes 98312 | tf_op jit(solution)/shard_map/ppermute | solution.py:21
  141.5 1.9 %collective-permute-start.9 = (bf16[32,512]{1,0:T(8,128)(2,1)S(1)}, bf16[32,512]{1,0:T(8,128)(2,1)S(1)}, u32[]{:S(2)}, u32[]{:S(2)}) collective-permute-start(bf16[32,512]{1,0:T(8,128)(2,1)S(1)} %get-tuple-element.4), channel_id=1, source_target_pairs={{4,0},{8,4},{12,8},{16,12},{20,16},{24,20},{28,24},{5,1},{9,5},{13... | collective-permute-start | bytes 98312 | tf_op jit(solution)/shard_map/ppermute | solution.py:23
  143.4 0.5 fusion.44
  143.9 0.0 collective-permute-done.8
  143.9 3.7 %collective-permute-done.9 = bf16[32,512]{1,0:T(8,128)(2,1)S(1)} collective-permute-done((bf16[32,512]{1,0:T(8,128)(2,1)S(1)}, bf16[32,512]{1,0:T(8,128)(2,1)S(1)}, u32[]{:S(2)}, u32[]{:S(2)}) %collective-permute-start.9) | collective-permute-done | bytes 32800 | tf_op jit(solution)/shard_map/ppermute | solution.py:23
  147.6 1.1 fusion.3
  (28 shorter events, 0.2 us)
Async XLA Ops:
  0.6 6.9 %copy-start = (bf16[1024,1024]{1,0:T(8,128)(2,1)S(1)}, bf16[1024,1024]{1,0:T(8,128)(2,1)}, u32[]{:S(2)}) copy-start(bf16[1024,1024]{1,0:T(8,128)(2,1)} %param.13) | copy-start | bytes 6291460
  0.6 11.1 %copy-start.4 = (f32[32,1024]{1,0:T(8,128)S(1)}, f32[32,1024]{1,0:T(8,128)}, u32[]{:S(2)}) copy-start(f32[32,1024]{1,0:T(8,128)} %param.11) | copy-start | bytes 393220
  0.7 7.3 %copy-start.9 = (s32[1,1024]{1,0:T(1,128)S(1)}, s32[1,1024]{1,0:T(1,128)}, u32[]{:S(2)}) copy-start(s32[1,1024]{1,0:T(1,128)} %param.16) | copy-start | bytes 12292
  0.7 11.1 %copy-start.5 = (f32[32,1024]{1,0:T(8,128)S(1)}, f32[32,1024]{1,0:T(8,128)}, u32[]{:S(2)}) copy-start(f32[32,1024]{1,0:T(8,128)} %param.12) | copy-start | bytes 393220
  1.7 7.0 %collective-permute-start = (bf16[32,512]{1,0:T(8,128)(2,1)S(1)}, bf16[32,512]{1,0:T(8,128)(2,1)S(1)}, u32[]{:S(2)}, u32[]{:S(2)}) collective-permute-start(bf16[32,512]{1,0:T(8,128)(2,1)S(1)} %get-tuple-element.11), channel_id=1, source_target_pairs={{0,4},{4,8},{8,12},{12,16},{16,20},{20,24},{24,28},{1,5},{5,9},{9,... | collective-permute-start | bytes 98312 | tf_op jit(solution)/shard_map/ppermute | solution.py:21
  5.4 12.7 %copy-start.3 = (bf16[1024,192]{0,1:T(8,128)(2,1)S(1)}, bf16[1024,192]{0,1:T(8,128)(2,1)}, u32[]{:S(2)}) copy-start(bf16[1024,192]{0,1:T(8,128)(2,1)} %param.18) | copy-start | bytes 1179652
  5.4 6.3 %collective-permute-start.1 = (bf16[32,512]{1,0:T(8,128)(2,1)S(1)}, bf16[32,512]{1,0:T(8,128)(2,1)S(1)}, u32[]{:S(2)}, u32[]{:S(2)}) collective-permute-start(bf16[32,512]{1,0:T(8,128)(2,1)S(1)} %get-tuple-element.12), channel_id=1, source_target_pairs={{4,0},{8,4},{12,8},{16,12},{20,16},{24,20},{28,24},{5,1},{9,5},{13... | collective-permute-start | bytes 98312 | tf_op jit(solution)/shard_map/ppermute | solution.py:23
  8.0 20.9 %copy-start.6 = (bf16[192,384]{1,0:T(8,128)(2,1)S(1)}, bf16[192,384]{1,0:T(8,128)(2,1)}, u32[]{:S(2)}) copy-start(bf16[192,384]{1,0:T(8,128)(2,1)} %param.19) | copy-start | bytes 442372
  8.0 53.2 %copy-start.8 = (s32[1024]{0:T(1024)}, s32[1024]{0:T(1024)S(1)}, u32[]{:S(2)}) copy-start(s32[1024]{0:T(1024)S(1)} %fusion.27) | copy-start | bytes 12292
  8.7 55.8 %copy-start.10 = (pred[1024]{0:T(1024)(128)(4,1)}, pred[1024]{0:T(1024)(128)(4,1)S(1)}, u32[]{:S(2)}) copy-start(pred[1024]{0:T(1024)(128)(4,1)S(1)} %get-tuple-element.17) | copy-start | bytes 3076
  8.7 55.8 %copy-start.11 = (pred[1024]{0:T(1024)(128)(4,1)}, pred[1024]{0:T(1024)(128)(4,1)S(1)}, u32[]{:S(2)}) copy-start(pred[1024]{0:T(1024)(128)(4,1)S(1)} %get-tuple-element.18) | copy-start | bytes 3076
  13.8 47.2 %collective-permute-start.2 = (bf16[32,512]{1,0:T(8,128)(2,1)S(1)}, bf16[32,512]{1,0:T(8,128)(2,1)S(1)}, u32[]{:S(2)}, u32[]{:S(2)}) collective-permute-start(bf16[32,512]{1,0:T(8,128)(2,1)S(1)} %get-tuple-element.9), channel_id=1, source_target_pairs={{0,4},{4,8},{8,12},{12,16},{16,20},{20,24},{24,28},{1,5},{5,9},{9,... | collective-permute-start | bytes 98312 | tf_op jit(solution)/shard_map/ppermute | solution.py:21
  15.8 45.2 %collective-permute-start.3 = (bf16[32,512]{1,0:T(8,128)(2,1)S(1)}, bf16[32,512]{1,0:T(8,128)(2,1)S(1)}, u32[]{:S(2)}, u32[]{:S(2)}) collective-permute-start(bf16[32,512]{1,0:T(8,128)(2,1)S(1)} %get-tuple-element.10), channel_id=1, source_target_pairs={{4,0},{8,4},{12,8},{16,12},{20,16},{24,20},{28,24},{5,1},{9,5},{13... | collective-permute-start | bytes 98312 | tf_op jit(solution)/shard_map/ppermute | solution.py:23
  56.4 11.2 %all-to-all-start = ((bf16[4,32,384]{2,1,0:T(8,128)(2,1)}), bf16[4,32,384]{2,1,0:T(8,128)(2,1)}, u32[]{:S(2)}, u32[]{:S(2)}) async-start(bf16[4,32,384]{2,1,0:T(8,128)(2,1)} %bitcast.3), calls=%async_computation | async-start | bytes 196608 | tf_op jit(solution)/shard_map/all_to_all | solution.py:76
  69.0 11.5 %copy-start.1 = (bf16[1024,1024]{1,0:T(8,128)(2,1)S(1)}, bf16[1024,1024]{1,0:T(8,128)(2,1)}, u32[]{:S(2)}) copy-start(bf16[1024,1024]{1,0:T(8,128)(2,1)} %param.14) | copy-start | bytes 6291460
  69.2 7.5 %collective-permute-start.4 = (bf16[32,512]{1,0:T(8,128)(2,1)S(1)}, bf16[32,512]{1,0:T(8,128)(2,1)S(1)}, u32[]{:S(2)}, u32[]{:S(2)}) collective-permute-start(bf16[32,512]{1,0:T(8,128)(2,1)S(1)} %get-tuple-element.7), channel_id=1, source_target_pairs={{0,4},{4,8},{8,12},{12,16},{16,20},{20,24},{24,28},{1,5},{5,9},{9,... | collective-permute-start | bytes 98312 | tf_op jit(solution)/shard_map/ppermute | solution.py:21
  74.3 6.1 %collective-permute-start.5 = (bf16[32,512]{1,0:T(8,128)(2,1)S(1)}, bf16[32,512]{1,0:T(8,128)(2,1)S(1)}, u32[]{:S(2)}, u32[]{:S(2)}) collective-permute-start(bf16[32,512]{1,0:T(8,128)(2,1)S(1)} %get-tuple-element.8), channel_id=1, source_target_pairs={{4,0},{8,4},{12,8},{16,12},{20,16},{24,20},{28,24},{5,1},{9,5},{13... | collective-permute-start | bytes 98312 | tf_op jit(solution)/shard_map/ppermute | solution.py:23
  81.1 46.8 %collective-permute-start.6 = (bf16[32,512]{1,0:T(8,128)(2,1)S(1)}, bf16[32,512]{1,0:T(8,128)(2,1)S(1)}, u32[]{:S(2)}, u32[]{:S(2)}) collective-permute-start(bf16[32,512]{1,0:T(8,128)(2,1)S(1)} %get-tuple-element.5), channel_id=1, source_target_pairs={{0,4},{4,8},{8,12},{12,16},{16,20},{20,24},{24,28},{1,5},{5,9},{9,... | collective-permute-start | bytes 98312 | tf_op jit(solution)/shard_map/ppermute | solution.py:21
  83.1 44.8 %collective-permute-start.7 = (bf16[32,512]{1,0:T(8,128)(2,1)S(1)}, bf16[32,512]{1,0:T(8,128)(2,1)S(1)}, u32[]{:S(2)}, u32[]{:S(2)}) collective-permute-start(bf16[32,512]{1,0:T(8,128)(2,1)S(1)} %get-tuple-element.6), channel_id=1, source_target_pairs={{4,0},{8,4},{12,8},{16,12},{20,16},{24,20},{28,24},{5,1},{9,5},{13... | collective-permute-start | bytes 98312 | tf_op jit(solution)/shard_map/ppermute | solution.py:23
  123.4 12.3 %all-to-all-start.1 = ((bf16[4,32,384]{2,1,0:T(8,128)(2,1)}), bf16[4,32,384]{2,1,0:T(8,128)(2,1)S(1)}, u32[]{:S(2)}, u32[]{:S(2)}) async-start(bf16[4,32,384]{2,1,0:T(8,128)(2,1)} %bitcast.6), calls=%async_computation.1 | async-start | bytes 196608 | tf_op jit(solution)/shard_map/all_to_all | solution.py:76
  136.1 11.5 %copy-start.2 = (bf16[1024,1024]{1,0:T(8,128)(2,1)S(1)}, bf16[1024,1024]{1,0:T(8,128)(2,1)}, u32[]{:S(2)}) copy-start(bf16[1024,1024]{1,0:T(8,128)(2,1)} %param.14) | copy-start | bytes 6291460
  136.3 12.4 %copy-start.7 = (f32[32,1024]{1,0:T(8,128)}, f32[32,1024]{1,0:T(8,128)S(1)}, u32[]{:S(2)}) copy-start(f32[32,1024]{1,0:T(8,128)S(1)} %get-tuple-element.16) | copy-start | bytes 393220
  136.3 7.5 %collective-permute-start.8 = (bf16[32,512]{1,0:T(8,128)(2,1)S(1)}, bf16[32,512]{1,0:T(8,128)(2,1)S(1)}, u32[]{:S(2)}, u32[]{:S(2)}) collective-permute-start(bf16[32,512]{1,0:T(8,128)(2,1)S(1)} %get-tuple-element.3), channel_id=1, source_target_pairs={{0,4},{4,8},{8,12},{12,16},{16,20},{20,24},{24,28},{1,5},{5,9},{9,... | collective-permute-start | bytes 98312 | tf_op jit(solution)/shard_map/ppermute | solution.py:21
  141.5 6.1 %collective-permute-start.9 = (bf16[32,512]{1,0:T(8,128)(2,1)S(1)}, bf16[32,512]{1,0:T(8,128)(2,1)S(1)}, u32[]{:S(2)}, u32[]{:S(2)}) collective-permute-start(bf16[32,512]{1,0:T(8,128)(2,1)S(1)} %get-tuple-element.4), channel_id=1, source_target_pairs={{4,0},{8,4},{12,8},{16,12},{20,16},{24,20},{28,24},{5,1},{9,5},{13... | collective-permute-start | bytes 98312 | tf_op jit(solution)/shard_map/ppermute | solution.py:23
where the time goes:
time: 150 us; the launch traced here: 149 us
  blocking collectives  75.5 us (50%)
  starting transfers between devices  37.6 us (25%)
  matrix products  12.3 us (8%)
  waiting for transfers between devices  10.4 us (7%)
  local copies, waits for them, and re-layouts  9.37 us (6%)
  other arithmetic  1.8 us (1%)
  between operations  1.77 us (1%)
    psum x2, blocking collectives, body(): totals = lax.psum(partial_sums, 'sub')  54.8 us
    all_gather x2, blocking collectives, body(): lax.all_gather(coefficients, 'col', axis=0, tiled=True)  20.7 us
    ppermute x5, starting transfers between devices, with_halo(): lax.ppermute(tail, axis, [(i, (i + 1) % count) for i in range(ends)])  17.8 us
    ppermute x5, starting transfers between devices, with_halo(): lax.ppermute(head, axis, [((i + 1) % count, i) for i in range(ends)])  10.7 us
    ppermute x5, waiting for transfers between devices, with_halo(): lax.ppermute(head, axis, [((i + 1) % count, i) for i in range(ends)])  10.4 us
    all_to_all x2, starting transfers between devices, body(): lax.all_to_all(totals.astype(jnp.bfloat16), 'col', split_axis=0, concat_a...  9.1 us
    gather x4, local copies, waits for them, and re-layouts, body(): picked = jnp.take(border, ov_rows[0], axis=1)  7.14 us
    dot_general x2, matrix products, body(): fine_part = jnp.dot(local_rhs, inverse, preferred_element_type=jnp.float32)  6.03 us
  transfers between devices with their start and end apart: 12, of which 3 were waited for; matrix products, arithmetic and copies ran while one was open for 11% of the time, Pallas kernels for 0%

commit v1 on v0

v1 whole, which is shorter than its diff:
```python
import functools

import jax
import jax.numpy as jnp
from jax import lax
from jax.experimental import pallas as pl
from jax.experimental.pallas import tpu as pltpu
from jax.sharding import PartitionSpec as P

ITERS = 2

cubic_coef = 0.1
MESH = pl.DeviceIdType.MESH
F32 = jnp.float32
BF16 = jnp.bfloat16


def dot(a, b):
    return jnp.dot(a, b, preferred_element_type=F32)


def dot_nt(a, b):
    return lax.dot_general(a, b, (((1,), (1,)), ((), ())), preferred_element_type=F32)


def kernel(
    n, m,
    state_hbm, load_hbm, diag_hbm, rim_hbm, inv_hbm, ov_hbm, count_ref, basis_hbm, map_hbm,
    solution_ref, residual_ref,
    cur, load, diag, rim, inv, ov, basis, maps, invp, turned, zmap,
    sent, halo, part_out, part_in,
    local_sem, halo_send, halo_recv, map_send, map_recv, part_send, part_recv,
):
    me_s = lax.axis_index("sub")
    me_c = lax.axis_index("col")
    rows, width = cur.shape
    h = halo.shape[3]
    nc = basis.shape[1]
    per = nc // m
    slots = ov.shape[1]
    half = inv.shape[0] - slots

    def fetch(index, source, target):
        copy = pltpu.make_async_copy(source, target, local_sem.at[index])
        copy.start()
        return copy

    get_state = fetch(0, state_hbm, cur)
    get_map = fetch(1, map_hbm, maps.at[me_c])
    get_diag = fetch(2, diag_hbm, diag)
    get_rim = fetch(3, rim_hbm, rim)
    get_load = fetch(4, load_hbm, load)
    get_basis = fetch(5, basis_hbm, basis)
    get_ov = fetch(6, ov_hbm, ov)
    get_inv = fetch(7, inv_hbm, inv)

    barrier = pltpu.get_barrier_semaphore()
    for k in range(1, n):
        pl.semaphore_signal(barrier, inc=1, device_id={"sub": lax.rem(me_s + k, n)}, device_id_type=MESH)
    for k in range(1, m):
        pl.semaphore_signal(barrier, inc=1, device_id={"col": lax.rem(me_c + k, m)}, device_id_type=MESH)

    for e in range(2 * ITERS + 1):
        @pl.when(me_s == 0)
        def _():
            halo[e, 0] = jnp.zeros((rows, h), BF16)

        @pl.when(me_s == n - 1)
        def _():
            halo[e, 1] = jnp.zeros((rows, h), BF16)

    get_state.wait()
    sent[0] = cur[...].astype(BF16)
    get_map.wait()
    pl.semaphore_wait(barrier, n + m - 2)

    def to_next(e):
        return pltpu.make_async_remote_copy(
            src_ref=sent.at[e, :, pl.ds(width - h, h)], dst_ref=halo.at[e, 0],
            send_sem=halo_send.at[e, 0], recv_sem=halo_recv.at[e, 0],
            device_id={"sub": lax.rem(me_s + 1, n)}, device_id_type=MESH)

    def to_prev(e):
        return pltpu.make_async_remote_copy(
            src_ref=sent.at[e, :, pl.ds(0, h)], dst_ref=halo.at[e, 1],
            send_sem=halo_send.at[e, 1], recv_sem=halo_recv.at[e, 1],
            device_id={"sub": lax.rem(me_s + n - 1, n)}, device_id_type=MESH)

    def halo_start(e):
        @pl.when(me_s < n - 1)
        def _():
            to_next(e).start()

        @pl.when(me_s > 0)
        def _():
            to_prev(e).start()

    def halo_wait(e):
        @pl.when(me_s > 0)
        def _():
            to_next(e).wait_recv()

        @pl.when(me_s < n - 1)
        def _():
            to_prev(e).wait_recv()

    def halo_done(e):
        @pl.when(me_s < n - 1)
        def _():
            to_next(e).wait_send()

        @pl.when(me_s > 0)
        def _():
            to_prev(e).wait_send()

    def map_copy(peer, slot):
        return pltpu.make_async_remote_copy(
            src_ref=maps.at[slot], dst_ref=maps.at[slot],
            send_sem=map_send.at[peer], recv_sem=map_recv.at[slot],
            device_id={"col": peer}, device_id_type=MESH)

    def part_copy(it, peer, slot):
        return pltpu.make_async_remote_copy(
            src_ref=part_out.at[it, peer], dst_ref=part_in.at[it, slot],
            send_sem=part_send.at[it, peer], recv_sem=part_recv.at[it, slot],
            device_id={"sub": peer}, device_id_type=MESH)

    halo_start(0)
    for k in range(1, m):
        map_copy(lax.rem(me_c + k, m), me_c).start()

    def residual(e, first):
        if first:
            get_diag.wait()
        acc = dot(sent[e], diag[...])
        if first:
            get_rim.wait()
            get_load.wait()
        halo_wait(e)
        acc = acc + dot(halo[e, 0], rim[:h]) + dot(halo[e, 1], rim[h:])
        v = cur[...]
        return load[...] - acc - cubic_coef * v * v * v

    def turn_map():
        across = n * per
        eye = (
            lax.broadcasted_iota(jnp.int32, (across, across), 0)
            == lax.broadcasted_iota(jnp.int32, (across, across), 1)
        ).astype(F32).astype(BF16)
        for a in range(m):
            turned[a] = dot_nt(eye, maps[a])
        for s in range(n):
            zmap[s] = jnp.concatenate(
                [turned[a, s * per : (s + 1) * per, :] for a in range(m)], axis=0
            ).astype(BF16)

    def partials(it, coefficients):
        for s in range(n):
            part_out[it, s] = dot_nt(coefficients, zmap[s]).astype(BF16)
        for k in range(1, n):
            part_copy(it, lax.rem(me_s + k, n), me_s).start()
        part_in[it, me_s] = part_out[it, me_s]

    def permuted_inverse():
        used = ov[...]
        slot = lax.broadcasted_iota(jnp.int32, used.shape, 1)
        used = jnp.where(slot < count_ref[0], used, -1)
        chunk = 256

        def step(i, carry):
            at = i * chunk
            place = lax.broadcasted_iota(jnp.int32, (chunk, slots), 0) + at
            pick = (place == used).astype(F32).astype(BF16)
            invp[pl.ds(pl.multiple_of(at, chunk), chunk), :] = dot(pick, inv[half:, :]).astype(BF16)
            return carry

        lax.fori_loop(0, 2 * h // chunk, step, 0)

    for it in range(ITERS):
        first = it == 0
        rb = residual(2 * it, first).astype(BF16)
        e = 2 * it + 1
        sent[e] = rb
        halo_start(e)
        if first:
            get_basis.wait()
        coefficients = dot(rb, basis[...]).astype(BF16)
        if not first:
            partials(it, coefficients)
        if first:
            get_inv.wait()
            get_ov.wait()
            permuted_inverse()
        fine = dot(rb, inv[:half, :])
        halo_wait(e)
        fine = fine + dot(halo[e, 0], invp[:h, :]) + dot(halo[e, 1], invp[h:, :])
        if first:
            for k in range(1, m):
                map_copy(me_c, lax.rem(me_c + k, m)).wait_recv()
            turn_map()
            partials(it, coefficients)
        for k in range(1, n):
            part_copy(it, me_s, lax.rem(me_s + k, n)).wait_recv()
        total = part_in[it, 0].astype(F32)
        for s in range(1, n):
            total = total + part_in[it, s].astype(F32)
        lift = dot_nt(total.astype(BF16), basis[...])
        v = cur[...] + (fine + lift)
        cur[...] = v
        sent[e + 1] = v.astype(BF16)
        halo_start(e + 1)

    solution_ref[...] = cur[...]
    residual_ref[...] = residual(2 * ITERS, False)

    for e in range(2 * ITERS + 1):
        halo_done(e)
    for k in range(1, m):
        map_copy(lax.rem(me_c + k, m), me_c).wait_send()
    for it in range(ITERS):
        for k in range(1, n):
            part_copy(it, lax.rem(me_s + k, n), me_s).wait_send()


def body(n, m, state_init, load_cols, stiff_diag, stiff_rim, inverse, ov_rows, ov_count, coarse_basis, coarse_map):
    rows, width = state_init.shape
    h = stiff_rim.shape[0] // 2
    nc = coarse_basis.shape[1]
    trades = 2 * ITERS + 1
    hbm = pl.BlockSpec(memory_space=pl.ANY)
    vmem = pl.BlockSpec(memory_space=pltpu.VMEM)
    smem = pl.BlockSpec(memory_space=pltpu.SMEM)
    dma = pltpu.SemaphoreType.DMA
    out = jax.ShapeDtypeStruct((rows, width), F32)
    return pl.pallas_call(
        functools.partial(kernel, n, m),
        out_shape=(out, out),
        in_specs=[hbm, hbm, hbm, hbm, hbm, hbm, smem, hbm, hbm],
        out_specs=(vmem, vmem),
        scratch_shapes=[
            pltpu.VMEM((rows, width), F32),
            pltpu.VMEM((rows, width), F32),
            pltpu.VMEM(stiff_diag.shape, BF16),
            pltpu.VMEM(stiff_rim.shape, BF16),
            pltpu.VMEM(inverse.shape, BF16),
            pltpu.VMEM(ov_rows.shape, jnp.int32),
            pltpu.VMEM(coarse_basis.shape, BF16),
            pltpu.VMEM((m,) + coarse_map.shape, BF16),
            pltpu.VMEM((2 * h, width), BF16),
            pltpu.VMEM((m, coarse_map.shape[1], nc), F32),
            pltpu.VMEM((n, nc, nc), BF16),
            pltpu.VMEM((trades, rows, width), BF16),
            pltpu.VMEM((trades, 2, rows, h), BF16),
            pltpu.VMEM((ITERS, n, rows, nc), BF16),
            pltpu.VMEM((ITERS, n, rows, nc), BF16),
            dma((8,)),
            dma((trades, 2)),
            dma((trades, 2)),
            dma((m,)),
            dma((m,)),
            dma((ITERS, n)),
            dma((ITERS, n)),
        ],
        compiler_params=pltpu.CompilerParams(collective_id=0, has_side_effects=True),
        name="schwarz",
    )(state_init, load_cols, stiff_diag, stiff_rim, inverse, ov_rows, ov_count, coarse_basis, coarse_map)


def solution(mesh):
    in_specs = (
        P("col", "sub"),
        P("col", "sub"),
        P(None, "sub"),
        P(None, "sub"),
        P(None, "sub"),
        P("sub", None),
        P("sub"),
        P("sub", None),
        P("sub", "col"),
    )
    out_specs = (P("col", "sub"), P("col", "sub"))
    step = functools.partial(body, mesh.shape["sub"], mesh.shape["col"])
    return jax.shard_map(step, mesh=mesh, in_specs=in_specs, out_specs=out_specs, check_vma=False)
```

time: 150 us -> 42.1 us (0.28)
  the two profiles are of different devices: /device:TPU:11 before, /device:TPU:9 now
where the time goes in v1:
time: 42.1 us; the launch traced here: 41.9 us
  Pallas kernels  35.5 us (84%)
  local copies, waits for them, and re-layouts  5.12 us (12%)
  between operations  1.29 us (3%)
    pallas_call x1, Pallas kernels, body(): pl.pallas_call(functools.partial(kernel, n, m), out_shape=(out, out), in_...  35.5 us
    unnamed x3, local copies, waits for them, and re-layouts  5.12 us

profile of v1, /device:TPU:9, one launch (start us, length us, event | category | flops | bytes accessed | tf_op | source)
XLA Modules:
  0.0 41.9 jit_solution(16187194016592227124)
XLA Ops:
  1.3 2.0 %copy.11.basis_hbm = bf16[1024,192]{1,0:T(8,128)(2,1)} copy(bf16[1024,192]{0,1:T(8,128)(2,1)} %param.16) | data formatting | bytes 786432 | tf_op args[7]
  3.3 35.5 %schwarz.1 = (f32[32,1024]{1,0:T(8,128)}, f32[32,1024]{1,0:T(8,128)}) custom-call(f32[32,1024]{1,0:T(8,128)} %state_hbm.1, f32[32,1024]{1,0:T(8,128)} %load_hbm.1, bf16[1024,1024]{1,0:T(8,128)(2,1)} %diag_hbm.1, bf16[1024,1024]{1,0:T(8,128)(2,1)} %rim_hbm.1, bf16[2048,1024]{1,0:T(8,128)(2,1)} %inv_hbm.1, s32[1,1024]{1,0:T(1,128)} %ov_hbm.1, ...), custom_call_target="tpu_custom_call" | custom-call | tf_op jit(solution)/shard_map/schwarz/pallas_call | solution.py:235
  38.8 1.6 %copy.15 = f32[32,1024]{1,0:T(8,128)} copy(f32[32,1024]{1,0:T(8,128)} %get-tuple-element.4) | data formatting | bytes 262144
  40.4 1.6 %copy.16 = f32[32,1024]{1,0:T(8,128)} copy(f32[32,1024]{1,0:T(8,128)} %get-tuple-element.5) | data formatting | bytes 262144

commit v2 on v1

v2 whole, which is shorter than its diff:
```python
import functools

import jax
import jax.numpy as jnp
from jax import lax
from jax.experimental import pallas as pl
from jax.experimental.pallas import tpu as pltpu
from jax.sharding import PartitionSpec as P

ITERS = 2
PIECES = 4

cubic_coef = 0.1
MESH = pl.DeviceIdType.MESH
F32 = jnp.float32
BF16 = jnp.bfloat16


def dot(a, b):
    return jnp.dot(a, b, preferred_element_type=F32)


def diagonal(size):
    place = [lax.broadcasted_iota(jnp.int32, (size, size), axis) for axis in (0, 1)]
    return (place[0] == place[1]).astype(F32).astype(BF16)


def dot_nt(a, b):
    return lax.dot_general(a, b, (((1,), (1,)), ((), ())), preferred_element_type=F32)


def kernel(
    n, m,
    state_hbm, load_hbm, diag_hbm, rim_hbm, inv_hbm, ov_hbm, count_hbm, basis_hbm, map_hbm,
    before_ref, change_ref, applied_ref,
    cur, load, diag, rim, inv, ov, count, basis, upright, maps, invp, turned, zmap,
    sent, halo, part_out, part_in,
    local_sem, halo_send, halo_recv, map_send, map_recv, relay_send, part_send, part_recv,
):
    me_s = lax.axis_index("sub")
    me_c = lax.axis_index("col")
    rows, width = cur.shape
    h = halo.shape[3]
    nc = basis.shape[0]
    per = nc // m
    slots = ov.shape[1]
    half = inv.shape[0] - slots

    barrier = pltpu.get_barrier_semaphore()
    for k in range(1, n):
        pl.semaphore_signal(barrier, inc=1, device_id={"sub": lax.rem(me_s + k, n)}, device_id_type=MESH)
    for k in range(1, m):
        pl.semaphore_signal(barrier, inc=1, device_id={"col": lax.rem(me_c + k, m)}, device_id_type=MESH)

    def fetch(index, source, target):
        copy = pltpu.make_async_copy(source, target, local_sem.at[index])
        copy.start()
        return copy

    get_state = fetch(0, state_hbm, cur)
    get_map = fetch(1, map_hbm, maps.at[me_c])
    get_diag = fetch(2, diag_hbm, diag)
    get_rim = fetch(3, rim_hbm, rim)
    get_load = fetch(4, load_hbm, load)
    get_basis = fetch(5, basis_hbm, basis)
    get_ov = fetch(6, ov_hbm, ov)
    get_count = fetch(7, count_hbm, count)
    get_inv = fetch(8, inv_hbm, inv)

    for e in range(2 * ITERS + 1):
        @pl.when(me_s == 0)
        def _():
            halo[e, 0] = jnp.zeros((rows, h), BF16)

        @pl.when(me_s == n - 1)
        def _():
            halo[e, 1] = jnp.zeros((rows, h), BF16)

    get_state.wait()
    sent[0] = cur[...].astype(BF16)
    get_map.wait()
    pl.semaphore_wait(barrier, n + m - 2)

    def to_next(e):
        return pltpu.make_async_remote_copy(
            src_ref=sent.at[e, :, pl.ds(width - h, h)], dst_ref=halo.at[e, 0],
            send_sem=halo_send.at[e, 0], recv_sem=halo_recv.at[e, 0],
            device_id={"sub": lax.rem(me_s + 1, n)}, device_id_type=MESH)

    def to_prev(e):
        return pltpu.make_async_remote_copy(
            src_ref=sent.at[e, :, pl.ds(0, h)], dst_ref=halo.at[e, 1],
            send_sem=halo_send.at[e, 1], recv_sem=halo_recv.at[e, 1],
            device_id={"sub": lax.rem(me_s + n - 1, n)}, device_id_type=MESH)

    def halo_start(e):
        @pl.when(me_s < n - 1)
        def _():
            to_next(e).start()

        @pl.when(me_s > 0)
        def _():
            to_prev(e).start()

    def halo_wait(e):
        @pl.when(me_s > 0)
        def _():
            to_next(e).wait_recv()

        @pl.when(me_s < n - 1)
        def _():
            to_prev(e).wait_recv()

    def halo_done(e):
        @pl.when(me_s < n - 1)
        def _():
            to_next(e).wait_send()

        @pl.when(me_s > 0)
        def _():
            to_prev(e).wait_send()

    relayed = m >= 4 and nc % (16 * PIECES) == 0
    pieces = PIECES if relayed else 1
    tall = nc // pieces
    upper = (2 * me_c) // m

    def map_copy(peer, slot, piece):
        return pltpu.make_async_remote_copy(
            src_ref=maps.at[slot, pl.ds(piece * tall, tall), :],
            dst_ref=maps.at[slot, pl.ds(piece * tall, tall), :],
            send_sem=map_send.at[peer, piece], recv_sem=map_recv.at[slot, piece],
            device_id={"col": peer}, device_id_type=MESH)

    def relay_copy(peer, slot, piece):
        return pltpu.make_async_remote_copy(
            src_ref=maps.at[slot, pl.ds(piece * tall, tall), :],
            dst_ref=maps.at[slot, pl.ds(piece * tall, tall), :],
            send_sem=relay_send.at[piece], recv_sem=map_recv.at[slot, piece],
            device_id={"col": peer}, device_id_type=MESH)

    def own_maps(act):
        for gap in range(m - 1 - relayed, 0, -1):
            for piece in range(pieces):
                @pl.when(me_c >= gap)
                def _():
                    act(map_copy(me_c - gap, me_c, piece))

                @pl.when(me_c + gap < m)
                def _():
                    act(map_copy(me_c + gap, me_c, piece))

    def relay(piece):
        if relayed:
            @pl.when(me_c == 1)
            def _():
                map_copy(1, m - 1, piece).wait_recv()
                relay_copy(0, m - 1, piece).start()

            @pl.when(me_c == m - 2)
            def _():
                map_copy(m - 2, 0, piece).wait_recv()
                relay_copy(m - 1, 0, piece).start()

    def relay_done():
        if relayed:
            for piece in range(pieces):
                @pl.when(me_c == 1)
                def _():
                    relay_copy(0, m - 1, piece).wait_send()

                @pl.when(me_c == m - 2)
                def _():
                    relay_copy(m - 1, 0, piece).wait_send()

    def part_copy(it, peer, slot):
        return pltpu.make_async_remote_copy(
            src_ref=part_out.at[it, peer], dst_ref=part_in.at[it, slot],
            send_sem=part_send.at[it, peer], recv_sem=part_recv.at[it, slot],
            device_id={"sub": peer}, device_id_type=MESH)

    halo_start(0)
    own_maps(lambda copy: copy.start())
    get_diag.wait()

    def stand_basis():
        block = 256
        for at in range(0, width, block):
            upright[at : at + block, :] = dot_nt(diagonal(block), basis[:, at : at + block]).astype(BF16)

    def applied(e, first):
        acc = dot(sent[e], diag[...])
        if first:
            get_basis.wait()
            stand_basis()
            get_rim.wait()
        halo_wait(e)
        return acc + dot(halo[e, 0], rim[:h]) + dot(halo[e, 1], rim[h:])

    def residual(e, first):
        acc = applied(e, first)
        if first:
            get_load.wait()
        v = cur[...]
        return load[...] - acc - cubic_coef * v * v * v

    def turn(j):
        flipped = dot_nt(diagonal(n * per), maps[j])
        if per % 16 == 0:
            for s in range(n):
                zmap[s, pl.ds(pl.multiple_of(j * per, 16), per), :] = flipped[s * per : (s + 1) * per].astype(BF16)
        else:
            turned[j] = flipped

    def turn_maps():
        for i in range(m):
            j = upper * (m - 1 - i) + (1 - upper) * i
            early = (me_c == 1) & (j == m - 1) | (me_c == m - 2) & (j == 0) if relayed else me_c < 0

            @pl.when((j != me_c) & jnp.logical_not(early))
            def _():
                for piece in range(pieces):
                    map_copy(me_c, j, piece).wait_recv()

            turn(j)
        if per % 16:
            for s in range(n):
                zmap[s] = jnp.concatenate(
                    [turned[a, s * per : (s + 1) * per, :] for a in range(m)], axis=0
                ).astype(BF16)

    def partials(it, coefficients):
        for s in range(n):
            part_out[it, s] = dot_nt(coefficients, zmap[s]).astype(BF16)
        for k in range(1, n):
            part_copy(it, lax.rem(me_s + k, n), me_s).start()
        part_in[it, me_s] = part_out[it, me_s]

    def permuted_inverse():
        used = ov[...]
        slot = lax.broadcasted_iota(jnp.int32, used.shape, 1)
        used = jnp.where(slot < count[0], used, -1)
        chunk = 2 * h // 4
        for i in range(4):
            place = lax.broadcasted_iota(jnp.int32, (chunk, slots), 0) + i * chunk
            pick = (place == used).astype(F32).astype(BF16)
            invp[i * chunk : (i + 1) * chunk, :] = dot(pick, inv[half:, :]).astype(BF16)
            if i == 1 and pieces > 1:
                relay(1)

    for it in range(ITERS):
        first = it == 0
        rb = residual(2 * it, first).astype(BF16)
        e = 2 * it + 1
        sent[e] = rb
        halo_start(e)
        coefficients = dot(rb, upright[...]).astype(BF16)
        if not first:
            partials(it, coefficients)
        if first:
            relay(0)
            get_inv.wait()
            get_ov.wait()
            get_count.wait()
            permuted_inverse()
        fine = dot(rb, inv[:half, :])
        halo_wait(e)
        fine = fine + dot(halo[e, 0], invp[:h, :]) + dot(halo[e, 1], invp[h:, :])
        if first:
            for piece in range(2, pieces):
                relay(piece)
            turn_maps()
            partials(it, coefficients)
        for k in range(1, n):
            part_copy(it, me_s, lax.rem(me_s + k, n)).wait_recv()
        total = part_in[it, 0].astype(F32)
        for s in range(1, n):
            total = total + part_in[it, s].astype(F32)
        lift = dot(total.astype(BF16), basis[...])
        change = fine + lift
        v = cur[...] + change
        if it == ITERS - 1:
            before_ref[...] = cur[...]
            change_ref[...] = change
        else:
            cur[...] = v
        sent[e + 1] = v.astype(BF16)
        halo_start(e + 1)

    applied_ref[...] = applied(2 * ITERS, False)

    for e in range(2 * ITERS + 1):
        halo_done(e)
    own_maps(lambda copy: copy.wait_send())
    relay_done()
    for it in range(ITERS):
        for k in range(1, n):
            part_copy(it, lax.rem(me_s + k, n), me_s).wait_send()


def body(n, m, state_init, load_cols, stiff_diag, stiff_rim, inverse, ov_rows, ov_count, coarse_basis, coarse_map):
    rows, width = state_init.shape
    h = stiff_rim.shape[0] // 2
    basis_t = coarse_basis.T
    nc = basis_t.shape[0]
    trades = 2 * ITERS + 1
    hbm = pl.BlockSpec(memory_space=pl.ANY)
    vmem = pl.BlockSpec(memory_space=pltpu.VMEM)
    dma = pltpu.SemaphoreType.DMA
    out = jax.ShapeDtypeStruct((rows, width), F32)
    before, change, product = pl.pallas_call(
        functools.partial(kernel, n, m),
        out_shape=(out, out, out),
        in_specs=[hbm] * 9,
        out_specs=(vmem, vmem, vmem),
        scratch_shapes=[
            pltpu.VMEM((rows, width), F32),
            pltpu.VMEM((rows, width), F32),
            pltpu.VMEM(stiff_diag.shape, BF16),
            pltpu.VMEM(stiff_rim.shape, BF16),
            pltpu.VMEM(inverse.shape, BF16),
            pltpu.VMEM(ov_rows.shape, jnp.int32),
            pltpu.SMEM((1,), jnp.int32),
            pltpu.VMEM(basis_t.shape, BF16),
            pltpu.VMEM(coarse_basis.shape, BF16),
            pltpu.VMEM((m,) + coarse_map.shape, BF16),
            pltpu.VMEM((2 * h, width), BF16),
            pltpu.VMEM((m, coarse_map.shape[1], nc), F32),
            pltpu.VMEM((n, nc, nc), BF16),
            pltpu.VMEM((trades, rows, width), BF16),
            pltpu.VMEM((trades, 2, rows, h), BF16),
            pltpu.VMEM((ITERS, n, rows, nc), BF16),
            pltpu.VMEM((ITERS, n, rows, nc), BF16),
            dma((9,)),
            dma((trades, 2)),
            dma((trades, 2)),
            dma((m, PIECES)),
            dma((m, PIECES)),
            dma((PIECES,)),
            dma((ITERS, n)),
            dma((ITERS, n)),
        ],
        compiler_params=pltpu.CompilerParams(collective_id=0, has_side_effects=True),
        name="schwarz",
    )(state_init, load_cols, stiff_diag, stiff_rim, inverse, ov_rows, ov_count, basis_t, coarse_map)
    current = before + change
    return current, load_cols - product - cubic_coef * current * current * current


def solution(mesh):
    in_specs = (
        P("col", "sub"),
        P("col", "sub"),
        P(None, "sub"),
        P(None, "sub"),
        P(None, "sub"),
        P("sub", None),
        P("sub"),
        P("sub", None),
        P("sub", "col"),
    )
    out_specs = (P("col", "sub"), P("col", "sub"))
    step = functools.partial(body, mesh.shape["sub"], mesh.shape["col"])
    return jax.shard_map(step, mesh=mesh, in_specs=in_specs, out_specs=out_specs, check_vma=False)
```

time: 42.1 us -> 37.5 us (0.89)
  the two profiles are of different devices: /device:TPU:9 before, /device:TPU:1 now
where the time goes in v2:
time: 37.5 us; the launch traced here: 37.4 us
  Pallas kernels  34.3 us (91%)
  other arithmetic  1.76 us (5%)
  between operations  1.3 us (3%)
    pallas_call x1, Pallas kernels, body(): pl.pallas_call(functools.partial(kernel, n, m), out_shape=(out, out, out)...  34.3 us
    sub x1, other arithmetic, body(): load_cols - product - cubic_coef * current * current * current  1.76 us

profile of v2, /device:TPU:1, one launch (start us, length us, event | category | flops | bytes accessed | tf_op | source)
XLA Modules:
  0.0 37.4 jit_solution(16574534057771291895)
XLA Ops:
  1.3 0.0 copy-start
  1.3 34.3 %schwarz.1 = (f32[32,1024]{1,0:T(8,128)}, f32[32,1024]{1,0:T(8,128)}, f32[32,1024]{1,0:T(8,128)}) custom-call(f32[32,1024]{1,0:T(8,128)} %state_hbm.1, f32[32,1024]{1,0:T(8,128)} %load_hbm.1, bf16[1024,1024]{1,0:T(8,128)(2,1)} %diag_hbm.1, bf16[1024,1024]{1,0:T(8,128)(2,1)} %rim_hbm.1, bf16[2048,1024]{1,0:T(8,128)(2,1)} %inv_hbm.1, s32[1,1024]{1,0:T(1,128)} %ov_hbm.1, ...), custom_call_target="tpu_custom_call" | custom-call | tf_op jit(solution)/shard_map/schwarz/pallas_call | solution.py:311
  35.6 0.0 copy-done
  35.6 1.8 %fusion = (f32[32,1024]{1,0:T(8,128)}, f32[32,1024]{1,0:T(8,128)}) fusion(f32[32,1024]{1,0:T(8,128)S(1)} %copy-done, f32[32,1024]{1,0:T(8,128)} %get-tuple-element.7, f32[32,1024]{1,0:T(8,128)} %get-tuple-element.5, f32[32,1024]{1,0:T(8,128)} %get-tuple-element.6), kind=kLoop, calls=%fused_computation.1 | loop fusion | flops 196608 | bytes 786432 | tf_op jit(solution)/shard_map/sub | solution.py:347
Async XLA Ops:
  1.3 34.3 %copy-start = (f32[32,1024]{1,0:T(8,128)S(1)}, f32[32,1024]{1,0:T(8,128)}, u32[]{:S(2)}) copy-start(f32[32,1024]{1,0:T(8,128)} %load_hbm.1) | copy-start | bytes 393220

commit v3 on v2

--- a/solution.py
+++ b/solution.py
@@ -14,6 +14,28 @@
 MESH = pl.DeviceIdType.MESH
 F32 = jnp.float32
 BF16 = jnp.bfloat16
+
+
+def packed_shape(rows, nc):
+    return (rows * nc // 128, 128) if nc % 128 == 64 and rows % 32 == 0 else (rows, nc)
+
+
+def pack(block):
+    rows, nc = block.shape
+    if packed_shape(rows, nc) == block.shape:
+        return block
+    full = nc - nc % 128
+    tail = jnp.concatenate([block[: rows // 2, full:], block[rows // 2 :, full:]], axis=1)
+    return jnp.concatenate([block[:, at : at + 128] for at in range(0, full, 128)] + [tail], axis=0)
+
+
+def unpack(block, rows, nc):
+    if packed_shape(rows, nc) == (rows, nc):
+        return block
+    count = nc // 128
+    tail = block[rows * count :]
+    tail = jnp.concatenate([tail[:, :64], tail[:, 64:]], axis=0)
+    return jnp.concatenate([block[rows * i : rows * (i + 1)] for i in range(count)] + [tail], axis=1)
 
 
 def dot(a, b):
@@ -231,7 +253,7 @@
 
     def partials(it, coefficients):
         for s in range(n):
-            part_out[it, s] = dot_nt(coefficients, zmap[s]).astype(BF16)
+            part_out[it, s] = pack(dot_nt(coefficients, zmap[s])).astype(BF16)
         for k in range(1, n):
             part_copy(it, lax.rem(me_s + k, n), me_s).start()
         part_in[it, me_s] = part_out[it, me_s]
@@ -276,7 +298,7 @@
         total = part_in[it, 0].astype(F32)
         for s in range(1, n):
             total = total + part_in[it, s].astype(F32)
-        lift = dot(total.astype(BF16), basis[...])
+        lift = dot(unpack(total, rows, nc).astype(BF16), basis[...])
         change = fine + lift
         v = cur[...] + change
         if it == ITERS - 1:
@@ -304,7 +326,7 @@
     basis_t = coarse_basis.T
     nc = basis_t.shape[0]
     trades = 2 * ITERS + 1
-    hbm = pl.BlockSpec(memory_space=pl.ANY)
+    hbm = pl.BlockSpec(memory_space=pltpu.HBM)
     vmem = pl.BlockSpec(memory_space=pltpu.VMEM)
     dma = pltpu.SemaphoreType.DMA
     out = jax.ShapeDtypeStruct((rows, width), F32)
@@ -329,8 +351,8 @@
             pltpu.VMEM((n, nc, nc), BF16),
             pltpu.VMEM((trades, rows, width), BF16),
             pltpu.VMEM((trades, 2, rows, h), BF16),
-            pltpu.VMEM((ITERS, n, rows, nc), BF16),
-            pltpu.VMEM((ITERS, n, rows, nc), BF16),
+            pltpu.VMEM((ITERS, n) + packed_shape(rows, nc), BF16),
+            pltpu.VMEM((ITERS, n) + packed_shape(rows, nc), BF16),
             dma((9,)),
             dma((trades, 2)),
             dma((trades, 2)),

time: 37.5 us -> 37.3 us (level)
  no operation moved by 1% of the time
where the time goes in v3:
time: 37.3 us; the launch traced here: 37.1 us
  Pallas kernels  34.1 us (91%)
  other arithmetic  1.76 us (5%)
  between operations  1.3 us (3%)
    pallas_call x1, Pallas kernels, body(): pl.pallas_call(functools.partial(kernel, n, m), out_shape=(out, out, out)...  34.1 us
    sub x1, other arithmetic, body(): load_cols - product - cubic_coef * current * current * current  1.76 us

profile of v3, /device:TPU:1, one launch (start us, length us, event | category | flops | bytes accessed | tf_op | source)
XLA Modules:
  0.0 37.1 jit_solution(11950596883703602484)
XLA Ops:
  1.3 0.0 copy-start
  1.3 34.1 %schwarz.1 = (f32[32,1024]{1,0:T(8,128)}, f32[32,1024]{1,0:T(8,128)}, f32[32,1024]{1,0:T(8,128)}) custom-call(f32[32,1024]{1,0:T(8,128)} %state_hbm.1, f32[32,1024]{1,0:T(8,128)} %load_hbm.1, bf16[1024,1024]{1,0:T(8,128)(2,1)} %diag_hbm.1, bf16[1024,1024]{1,0:T(8,128)(2,1)} %rim_hbm.1, bf16[2048,1024]{1,0:T(8,128)(2,1)} %inv_hbm.1, s32[1,1024]{1,0:T(1,128)} %ov_hbm.1, ...), custom_call_target="tpu_custom_call" | custom-call | tf_op jit(solution)/shard_map/schwarz/pallas_call | solution.py:333
  35.4 0.0 copy-done
  35.4 1.8 %fusion = (f32[32,1024]{1,0:T(8,128)}, f32[32,1024]{1,0:T(8,128)}) fusion(f32[32,1024]{1,0:T(8,128)S(1)} %copy-done, f32[32,1024]{1,0:T(8,128)} %get-tuple-element.7, f32[32,1024]{1,0:T(8,128)} %get-tuple-element.5, f32[32,1024]{1,0:T(8,128)} %get-tuple-element.6), kind=kLoop, calls=%fused_computation.1 | loop fusion | flops 196608 | bytes 786432 | tf_op jit(solution)/shard_map/sub | solution.py:369
Async XLA Ops:
  1.3 34.1 %copy-start = (f32[32,1024]{1,0:T(8,128)S(1)}, f32[32,1024]{1,0:T(8,128)}, u32[]{:S(2)}) copy-start(f32[32,1024]{1,0:T(8,128)} %load_hbm.1) | copy-start | bytes 393220
